TPU v7x, 128 devices: a whole 4x4x4 slice. The times are simulated.
128 devices in a mesh: section: 8 (over x, z_hi), ctx: 16 (over z_lo, y, core).
Axes of the slice: x: 4, y: 4, z: 4 (z_hi: 2, z_lo: 2; z = z_hi * 2 + z_lo), core: 2. Of those that a mesh axis runs over, the one named last changes fastest.
Arguments:
- acts: bfloat16 [8, 2048, 12288], P('section', 'ctx'), may hold values from -6 to 6
- cots: bfloat16 [8, 2048, 4096], P('section', 'ctx'), may hold values from -1.1953125 to 1.1953125
- kern: float32 [8, 7, 12288], P('section'), may hold values from -2 to 2
- filt: bfloat16 [8, 4096, 2048], P('section', 'ctx'), may hold values from -9 to 9
- skip: float32 [8, 4096], P('section'), may hold values from 0.5 to 1.5
Outputs:
- output: bfloat16 [8, 2048, 4096], P('section', 'ctx')
- input_grad: bfloat16 [8, 2048, 12288], P('section', 'ctx')
- kern_grad: float32 [8, 7, 12288], P('section')
- filt_grad: float32 [8, 4096, 2048], P('section', 'ctx')
- skip_grad: float32 [8, 4096], P('section', 'ctx')
All inputs are finite; a program needn't handle non-finite values.
Results may differ from a plain program's by a relative error of at most 0.023.
Values may be sent and summed in bfloat16 or wider, within the bound.
No kernel may reach another device: no remote copies, remote signals or barrier semaphores. Data moves between devices by JAX's collectives and lax.ppermute only.
A program may use at most 192 MiB of HBM per device.

v0:
```python
import math
import jax
import jax.numpy as jnp
from jax import lax
from jax.sharding import PartitionSpec as P


def passed_along(value, axis, steps):
    count = lax.axis_size(axis)
    pairs = [(source, (source + steps) % count) for source in range(count)]
    return lax.ppermute(value, axis, pairs)


def from_behind(block, axis, distance):
    devices = range(lax.axis_size(axis))
    route = [(i - distance, i) for i in devices if i - distance in devices]
    return lax.ppermute(block, axis, route)


def factor_length(total):
    best = 2
    for divisor in range(2, math.isqrt(total) + 1):
        if total % divisor == 0 and divisor % 2 == 0:
            best = divisor
    return (best, total // best)


def phases(rows, cols, total):
    left = jnp.arange(rows, dtype=jnp.int32)[:, None]
    right = jnp.arange(cols, dtype=jnp.int32)[None, :]
    return (left * right % total).astype(jnp.float32) * (2.0 * math.pi / total)


def block_table(cos_t, sin_t, sign):
    top = jnp.stack([cos_t, sign * sin_t], axis=1)
    bottom = jnp.stack([-sign * sin_t, cos_t], axis=1)
    return jnp.stack([top, bottom], axis=0)


def make_tables(first, second):
    total = first * second
    outer = phases(first, first // 2, first)
    twist = phases(first, second, total)
    inner = phases(second, second, second)
    outer_pair = jnp.stack([jnp.cos(outer), -jnp.sin(outer)], axis=0)
    inner_cos = jnp.cos(inner)
    inner_sin = jnp.sin(inner)
    return (
        outer_pair,
        jnp.cos(twist),
        jnp.sin(twist),
        block_table(inner_cos, inner_sin, 1.0),
        block_table(inner_cos, inner_sin, -1.0),
    )


def contract(form, table, values):
    return jnp.einsum(form, table, values, precision=lax.Precision.HIGH)


def contract_narrow(form, table, values):
    upper = table.astype(jnp.bfloat16)
    lower = (table - upper.astype(jnp.float32)).astype(jnp.bfloat16)
    return jnp.einsum(form, upper, values, preferred_element_type=jnp.float32) + jnp.einsum(
        form, lower, values, preferred_element_type=jnp.float32
    )


def forward_transform(signal, tables):
    outer_pair, twist_cos, twist_sin, inner_fwd, inner_inv = tables
    first, second = twist_cos.shape
    columns = signal.shape[1]
    blocked = signal.reshape(first // 2, second, columns)
    spread = contract_narrow("pkm,mjc->pkjc", outer_pair, blocked)
    a_real = spread[0]
    a_imag = spread[1]
    b_real = a_real * twist_cos[:, :, None] + a_imag * twist_sin[:, :, None]
    b_imag = a_imag * twist_cos[:, :, None] - a_real * twist_sin[:, :, None]
    stacked = jnp.stack([b_real, b_imag], axis=0)
    return contract("pqsj,skjc->pkqc", inner_fwd, stacked)


def cmul(left, right, conj_right):
    if conj_right:
        return jnp.stack(
            [left[0] * right[0] + left[1] * right[1], left[1] * right[0] - left[0] * right[1]],
            axis=0,
        )
    return jnp.stack(
        [left[0] * right[0] - left[1] * right[1], left[0] * right[1] + left[1] * right[0]], axis=0
    )


def inverse_transform(spectrum, tables):
    outer_pair, twist_cos, twist_sin, inner_fwd, inner_inv = tables
    first, second = twist_cos.shape
    columns = spectrum.shape[3]
    back = contract("pjsq,skqc->pkjc", inner_inv, spectrum)
    g_real = back[0] * twist_cos[:, :, None] - back[1] * twist_sin[:, :, None]
    g_imag = back[0] * twist_sin[:, :, None] + back[1] * twist_cos[:, :, None]
    result = contract("skm,skjc->mjc", outer_pair, jnp.stack([g_real, g_imag], axis=0))
    return result.reshape(first // 2 * second, columns) / (first * second)


def on_device(acts, cots, kern, filt, skip):
    source = passed_along(acts, "section", 1)[0]
    incoming = passed_along(cots, "section", -1)[0]
    taps = kern.shape[1]
    margin = taps - 1
    tokens_dev, feats = source.shape
    width = feats // 3
    groups = lax.axis_size("ctx")
    chans = width // groups
    seq_len = tokens_dev * groups
    before = from_behind(source[tokens_dev - margin :], "ctx", 1)
    padded = jnp.concatenate([before, source], axis=0).astype(jnp.float32)
    weights = kern[0]
    feature = sum(
        (
            weights[offset][None, :] * padded[margin - offset : margin - offset + tokens_dev]
            for offset in range(taps)
        )
    )
    query = feature[:, :width]
    keyed = feature[:, width : 2 * width]
    value = feature[:, 2 * width :]
    gated = (keyed * value).astype(jnp.bfloat16)
    gain_all = skip[0]
    gain_part = lax.dynamic_slice_in_dim(gain_all, lax.axis_index("ctx") * chans, chans)
    first, second = factor_length(2 * seq_len)
    tables = make_tables(first, second)
    filt_spec = forward_transform(filt[0].T, tables)
    grad_in = incoming.astype(jnp.float32)
    grad_mix = (grad_in * query).astype(jnp.bfloat16)
    gated_part = lax.all_to_all(gated, "ctx", split_axis=1, concat_axis=0, tiled=True)
    gated_f = gated_part.astype(jnp.float32)
    gated_spec = forward_transform(gated_part, tables)
    mixed = inverse_transform(cmul(gated_spec, filt_spec, False), tables)
    mixed_part = mixed.astype(jnp.bfloat16)
    mixed_seq = lax.all_to_all(mixed_part, "ctx", split_axis=0, concat_axis=1, tiled=True)
    grad_part = lax.all_to_all(grad_mix, "ctx", split_axis=1, concat_axis=0, tiled=True)
    gated_f, gated_spec = (gated_f, gated_spec)
    grad_f = grad_part.astype(jnp.float32)
    grad_spec = forward_transform(grad_part, tables)
    back = inverse_transform(cmul(grad_spec, filt_spec, True), tables)
    filt_grad = inverse_transform(cmul(grad_spec, gated_spec, True), tables)
    through = (back + gain_part[None, :] * grad_f).astype(jnp.bfloat16)
    skip_grad = jnp.sum(grad_f * gated_f, axis=0)
    through_part, filt_grad, skip_grad = (through, filt_grad, skip_grad)
    through_seq = lax.all_to_all(through_part, "ctx", split_axis=0, concat_axis=1, tiled=True)
    inner = mixed_seq.astype(jnp.float32) + gain_all[None, :] * gated.astype(jnp.float32)
    output = (query * inner).astype(jnp.bfloat16)
    through_f = through_seq.astype(jnp.float32)
    feat_grad = jnp.concatenate([grad_in * inner, through_f * value, through_f * keyed], axis=1)
    after = from_behind(feat_grad[:margin].astype(jnp.bfloat16), "ctx", -1).astype(jnp.float32)
    extended = jnp.concatenate([feat_grad, after], axis=0)
    input_grad = sum(
        (
            weights[offset][None, :] * extended[offset : offset + tokens_dev]
            for offset in range(taps)
        )
    ).astype(jnp.bfloat16)
    partial_kern = jnp.sum(
        jnp.stack(
            [
                feat_grad * padded[margin - offset : margin - offset + tokens_dev]
                for offset in range(taps)
            ],
            axis=0,
        ),
        axis=1,
    )
    kern_grad = lax.psum(partial_kern.astype(jnp.bfloat16), "ctx").astype(jnp.float32)
    return (output[None], input_grad[None], kern_grad[None], filt_grad.T[None], skip_grad[None])


def solution(mesh):
    return jax.shard_map(
        on_device,
        mesh=mesh,
        in_specs=(
            P("section", "ctx", None),
            P("section", "ctx", None),
            P("section", None, None),
            P("section", "ctx", None),
            P("section", None),
        ),
        out_specs=(
            P("section", "ctx", None),
            P("section", "ctx", None),
            P("section", None, None),
            P("section", "ctx", None),
            P("section", "ctx"),
        ),
        check_vma=False,
    )
```

profile of v0, /device:TPU:25, one launch (start us, length us, event | category | flops | bytes accessed | tf_op | source)
XLA Modules:
  0.0 614.9 jit_solution(2262165847482371102)
XLA Ops:
  9.5 5.8 collective-permute-start.2
  22.4 82.2 %collective-permute-done = bf16[1,128,12288]{1,2,0:T(8,128)(2,1)} collective-permute-done((bf16[1,128,12288]{1,2,0:T(8,128)(2,1)}, bf16[1,128,12288]{1,2,0:T(8,128)(2,1)}, u32[]{:S(2)}, u32[]{:S(2)}) %collective-permute-start) | collective-permute-done | bytes 3145760 | tf_op jit(solution)/shard_map/ppermute | solution.py:11
  126.1 24.5 %multiply_add_fusion = f32[128,12288]{0,1:T(8,128)} fusion(f32[134,12288]{0,1:T(8,128)S(1)} %maximum_convert_fusion, f32[12288]{0:T(1024)S(1)} %bitcast.243, f32[12288]{0:T(1024)S(1)} %bitcast.245, f32[12288]{0:T(1024)S(1)} %bitcast.235, f32[12288]{0:T(1024)S(1)} %bitcast.237, f32[12288]{0:T(1024)S(1)} %bitcast.239, f32[12288]{0:T(1024)S(1)} %bitcast.241, ...), kind=kLoop, calls=%fused_computation.60 | loop fusion | flops 20447232 | bytes 50675712 | tf_op jit(solution)/shard_map/add | solution.py:118
  153.8 7.0 %all-to-all-start.2 = ((bf16[128,16,256]{0,2,1:T(8,128)(2,1)}), bf16[128,16,256]{0,2,1:T(8,128)(2,1)S(1)}, u32[]{:S(2)}, u32[]{:S(2)}) async-start(bf16[128,16,256]{0,2,1:T(8,128)(2,1)} %bitcast.232), calls=%async_computation.2 | async-start | bytes 2097152 | tf_op jit(solution)/shard_map/all_to_all | solution.py:141
  166.7 7.9 %all-to-all-done.2 = bf16[128,16,256]{0,2,1:T(8,128)(2,1)S(1)} async-done(((bf16[128,16,256]{0,2,1:T(8,128)(2,1)}), bf16[128,16,256]{0,2,1:T(8,128)(2,1)S(1)}, u32[]{:S(2)}, u32[]{:S(2)}) %all-to-all-start.2) | async-done | bytes 1048608 | tf_op jit(solution)/shard_map/all_to_all | solution.py:141
  178.8 7.3 %multiply_add_fusion.5 = (f32[1,64,64,256]{3,1,2,0:T(8,128)}, f32[1,64,64,256]{3,1,2,0:T(8,128)}, f32[1,64,64,256]{3,1,2,0:T(8,128)}, f32[1,64,64,256]{3,1,2,0:T(8,128)}) fusion(f32[2,64,64,256]{3,1,2,0:T(8,128)S(1)} %convolution_add_fusion, f32[64,64]{0,1:T(8,128)S(1)} %get-tuple-element.64, f32[64,64]{0,1:T(8,128)S(1)} %get-tuple-element.65, ...), kind=kLoop, calls=%fused_computation.70 | loop fusion | flops 12582912 | bytes 33587200 | tf_op jit(solution)/shard_map/add | solution.py:77
  194.3 8.5 %fusion.40 = f32[2,64,64,256]{3,2,0,1:T(8,128)S(1)} fusion(f32[2,64,64,256,1]{3,1,2,0,4:T(8,128)S(1)} %maximum_bitcast_fusion.4, f32[1,64,2,64]{3,1,2,0:T(8,128)S(1)} %get-tuple-element.57, f32[1,64,2,64]{3,1,2,0:T(8,128)S(1)} %get-tuple-element.60), kind=kOutput, calls=%fused_computation.84 | convolution fusion | flops 1610629120 | bytes 16842752 | tf_op jit(solution)/shard_map/pqsj,skjc->pkqc/dot_general | solution.py:58
  202.8 8.7 %fusion.37 = f32[2,64,64,256]{3,2,0,1:T(8,128)S(1)} fusion(f32[2,64,64,256,1]{3,1,2,0,4:T(8,128)S(1)} %maximum_bitcast_fusion.1, f32[1,64,2,64]{3,1,2,0:T(8,128)S(1)} %get-tuple-element.57, f32[1,64,2,64]{3,1,2,0:T(8,128)S(1)} %get-tuple-element.60), kind=kOutput, calls=%fused_computation.83 | convolution fusion | flops 1610629120 | bytes 16842752 | tf_op jit(solution)/shard_map/pqsj,skjc->pkqc/dot_general | solution.py:58
  217.3 6.5 %fusion.44 = f32[64,256,2,64]{1,3,2,0:T(8,128)S(1)} fusion(f32[1,64,64,256]{3,2,0,1:T(8,128)} %get-tuple-element.23, f32[1,64,64,256]{3,2,0,1:T(8,128)} %get-tuple-element.22, f32[1,64,2,64]{3,1,2,0:T(8,128)S(1)} %get-tuple-element.61, f32[1,64,2,64]{3,1,2,0:T(8,128)S(1)} %get-tuple-element.56), kind=kOutput, calls=%fused_computation.86 | convolution fusion | flops 1612726272 | bytes 16842752 | tf_op jit(solution)/shard_map/pjsq,skqc->pkjc/dot_general | solution.py:58
  238.0 19.4 %all_to_all.52 = bf16[16,128,256]{1,2,0:T(8,128)(2,1)S(1)} all-to-all(bf16[16,128,256]{1,2,0:T(8,128)(2,1)S(1)} %fusion.48), channel_id=1, replica_groups=mesh['section'=8,'ctx'=16] {'ctx'}, dimensions={0} | all-to-all | bytes 2097152 | tf_op jit(solution)/shard_map/all_to_all | solution.py:150
  262.3 20.2 %all_to_all.53 = bf16[128,16,256]{0,2,1:T(8,128)(2,1)} all-to-all(bf16[128,16,256]{0,2,1:T(8,128)(2,1)S(1)} %bitcast.220), channel_id=1, replica_groups=mesh['section'=8,'ctx'=16] {'ctx'}, dimensions={1} | all-to-all | bytes 2097152 | tf_op jit(solution)/shard_map/all_to_all | solution.py:135
  294.3 14.0 %fusion.34 = f32[2,64,64,256]{3,2,0,1:T(8,128)} fusion(f32[2,64,64,256,1]{3,1,2,0,4:T(8,128)} %maximum_bitcast_fusion, f32[1,64,2,64]{3,1,2,0:T(8,128)S(1)} %get-tuple-element.57, f32[1,64,2,64]{3,1,2,0:T(8,128)S(1)} %get-tuple-element.60), kind=kOutput, calls=%fused_computation.82 | convolution fusion | flops 1610629120 | bytes 16842752 | tf_op jit(solution)/shard_map/pqsj,skjc->pkqc/dot_general | solution.py:58
  308.3 11.9 %multiply_add_fusion.2 = (f32[1,64,64,256]{3,2,0,1:T(8,128)}, f32[1,64,64,256]{3,2,0,1:T(8,128)}, f32[1,64,64,256]{3,2,0,1:T(8,128)}, f32[1,64,64,256]{3,2,0,1:T(8,128)}) fusion(f32[2,64,64,256]{3,2,0,1:T(8,128)S(1)} %bitcast.212, f32[2,64,64,256]{3,2,0,1:T(8,128)} %fusion.34, f32[2,64,64,256]{3,2,0,1:T(8,128)} %copy-done.8), kind=kLoop, calls=%fused_computation.64 | loop fusion | flops 12582912 | bytes 41943040 | tf_op jit(solution)/shard_map/add | solution.py:86
  320.1 6.4 %fusion.45 = f32[64,256,2,64]{1,3,2,0:T(8,128)S(1)} fusion(f32[1,64,64,256]{3,2,0,1:T(8,128)} %get-tuple-element.38, f32[1,64,64,256]{3,2,0,1:T(8,128)} %get-tuple-element.39, f32[1,64,2,64]{3,1,2,0:T(8,128)S(1)} %get-tuple-element.61, f32[1,64,2,64]{3,1,2,0:T(8,128)S(1)} %get-tuple-element.56), kind=kOutput, calls=%fused_computation.87 | convolution fusion | flops 1612726272 | bytes 16842752 | tf_op jit(solution)/shard_map/pjsq,skqc->pkjc/dot_general | solution.py:58
  331.4 6.5 %fusion.43 = f32[64,256,2,64]{1,3,2,0:T(8,128)S(1)} fusion(f32[1,64,64,256]{3,2,0,1:T(8,128)} %get-tuple-element.21, f32[1,64,64,256]{3,2,0,1:T(8,128)} %get-tuple-element.20, f32[1,64,2,64]{3,1,2,0:T(8,128)S(1)} %get-tuple-element.61, f32[1,64,2,64]{3,1,2,0:T(8,128)S(1)} %get-tuple-element.56), kind=kOutput, calls=%fused_computation.85 | convolution fusion | flops 1612726272 | bytes 16842752 | tf_op jit(solution)/shard_map/pjsq,skqc->pkjc/dot_general | solution.py:58
  337.9 8.2 %copy.163 = f32[64,256,2,64]{1,0,3,2:T(8,128)} copy(f32[64,256,2,64]{1,3,2,0:T(8,128)S(1)} %fusion.43) | data formatting | bytes 16777216 | tf_op jit(solution)/shard_map/pjsq,skqc->pkjc/dot_general | solution.py:58
  346.1 7.9 %multiply_subtract_fusion = (f32[1,64,64,256]{3,1,2,0:T(8,128)}, f32[1,64,64,256]{3,1,2,0:T(8,128)}, f32[1,64,64,256]{3,1,2,0:T(8,128)S(1)}, f32[1,64,64,256]{3,1,2,0:T(8,128)}) fusion(f32[2,64,64,256]{3,1,2,0:T(8,128)} %bitcast.217, f32[64,64]{0,1:T(8,128)S(1)} %get-tuple-element.64, f32[64,64]{0,1:T(8,128)S(1)} %get-tuple-element.65, ...), kind=kLoop, calls=%fused_computation.62 | loop fusion | flops 12582912 | bytes 33587200 | tf_op jit(solution)/shard_map/sub | solution.py:99
  353.9 5.1 fusion.51
  360.6 6.6 %all-to-all-start.1 = ((bf16[16,128,256]{2,1,0:T(8,128)(2,1)}), bf16[16,128,256]{2,1,0:T(8,128)(2,1)}, u32[]{:S(2)}, u32[]{:S(2)}) async-start(bf16[16,128,256]{2,1,0:T(8,128)(2,1)} %bitcast.231), calls=%async_computation.1 | async-start | bytes 2097152 | tf_op jit(solution)/shard_map/all_to_all | solution.py:140
  367.3 5.3 bitcast_multiply_fusion
  390.7 6.7 %pad_maximum_fusion.1 = bf16[128,12288]{0,1:T(8,128)(2,1)} fusion(f32[128,4096]{0,1:T(8,128)S(1)} %copy-done.1, f32[128,4096]{0,1:T(8,128)S(1)} %get-tuple-element.40, f32[128,4096]{0,1:T(8,128)S(1)} %get-tuple-element.43), kind=kLoop, calls=%fused_computation.52 | loop fusion | flops 9437184 | bytes 9437184 | tf_op jit(solution)/shard_map/concatenate | solution.py:154
  397.4 10.1 %bitcast_dynamic-update-slice_fusion.6 = f32[7,128,12288]{1,2,0:T(8,128)} fusion(f32[134,12288]{0,1:T(8,128)} %copy-done, f32[128,4096]{0,1:T(8,128)S(1)} %copy-done.1, f32[128,4096]{0,1:T(8,128)S(1)} %get-tuple-element.40, f32[128,4096]{0,1:T(8,128)S(1)} %get-tuple-element.43), kind=kLoop, calls=%fused_computation.59 | loop fusion | flops 4718591 | bytes 18874368
  412.9 10.0 %bitcast_dynamic-update-slice_fusion.5 = f32[7,128,12288]{1,2,0:T(8,128)} fusion(f32[7,128,12288]{1,2,0:T(8,128)} %bitcast_dynamic-update-slice_fusion.6, f32[134,12288]{0,1:T(8,128)} %copy-done, f32[128,4096]{0,1:T(8,128)} %get-tuple-element.41, f32[128,4096]{0,1:T(8,128)S(1)} %get-tuple-element.40, f32[128,4096]{0,1:T(8,128)} %copy-done.4), kind=kLoop, calls=%fused_computation.58 | loop fusion | flops 4718592 | bytes 18874368
  422.9 10.3 %bitcast_dynamic-update-slice_fusion.4 = f32[7,128,12288]{1,2,0:T(8,128)} fusion(f32[7,128,12288]{1,2,0:T(8,128)} %bitcast_dynamic-update-slice_fusion.5, f32[134,12288]{0,1:T(8,128)} %copy-done, f32[128,4096]{0,1:T(8,128)S(1)} %copy-done.2, f32[128,4096]{0,1:T(8,128)S(1)} %get-tuple-element.40, f32[128,4096]{0,1:T(8,128)S(1)} %copy-done.5), kind=kLoop, calls=%fused_computation.57 | loop fusion | flops 4718592 | bytes 18874368
  433.2 7.4 %bitcast_dynamic-update-slice_fusion.3 = f32[7,128,12288]{1,2,0:T(8,128)} fusion(f32[7,128,12288]{1,2,0:T(8,128)} %bitcast_dynamic-update-slice_fusion.4, f32[134,12288]{0,1:T(8,128)S(1)} %bitcast.210, f32[128,4096]{0,1:T(8,128)S(1)} %copy-done.2, f32[128,4096]{0,1:T(8,128)S(1)} %get-tuple-element.40, f32[128,4096]{0,1:T(8,128)S(1)} %copy-done.5), kind=kLoop, calls=%fused_computation.56 | loop fusion | flops 4718592 | bytes 18874368
  440.6 7.3 %bitcast_dynamic-update-slice_fusion.2 = f32[7,128,12288]{1,2,0:T(8,128)} fusion(f32[7,128,12288]{1,2,0:T(8,128)} %bitcast_dynamic-update-slice_fusion.3, f32[134,12288]{0,1:T(8,128)S(1)} %bitcast.210, f32[128,4096]{0,1:T(8,128)S(1)} %copy-done.2, f32[128,4096]{0,1:T(8,128)S(1)} %get-tuple-element.40, f32[128,4096]{0,1:T(8,128)S(1)} %copy-done.5), kind=kLoop, calls=%fused_computation.55 | loop fusion | flops 4718592 | bytes 18874368
  447.8 7.6 %bitcast_dynamic-update-slice_fusion.1 = f32[7,128,12288]{1,2,0:T(8,128)} fusion(f32[7,128,12288]{1,2,0:T(8,128)} %bitcast_dynamic-update-slice_fusion.2, f32[134,12288]{0,1:T(8,128)S(1)} %bitcast.210, f32[128,4096]{0,1:T(8,128)S(1)} %copy-done.2, f32[128,4096]{0,1:T(8,128)S(1)} %get-tuple-element.40, f32[128,4096]{0,1:T(8,128)S(1)} %copy-done.5), kind=kLoop, calls=%fused_computation.54 | loop fusion | flops 4718592 | bytes 18874368
  455.4 7.2 %bitcast_dynamic-update-slice_fusion = f32[7,128,12288]{1,2,0:T(8,128)} fusion(f32[7,128,12288]{1,2,0:T(8,128)} %bitcast_dynamic-update-slice_fusion.1, f32[134,12288]{0,1:T(8,128)S(1)} %bitcast.210, f32[128,4096]{0,1:T(8,128)S(1)} %copy-done.2, f32[128,4096]{0,1:T(8,128)S(1)} %get-tuple-element.40, f32[128,4096]{0,1:T(8,128)S(1)} %copy-done.5), kind=kLoop, calls=%fused_computation.53 | loop fusion | flops 4718592 | bytes 18874368 | tf_op jit(solution)/shard_map/stack | solution.py:164
  463.9 20.5 %reduce_sum.18 = bf16[7,12288]{1,0:T(8,128)(2,1)S(1)} reduce(f32[7,128,12288]{1,2,0:T(8,128)} %bitcast_dynamic-update-slice_fusion, f32[]{:T(128)} %constant.55.clone.1), dimensions={1}, to_apply=%region_0.1 | reduce | flops 10924032 | bytes 44212228 | tf_op jit(solution)/shard_map/reduce_sum | solution.py:163
  489.0 12.3 %pad_maximum_fusion = f32[134,12288]{0,1:T(8,128)} fusion(f32[6,12288]{0,1:T(8,128)} %copy.94, f32[128,4096]{0,1:T(8,128)} %get-tuple-element.41, f32[128,4096]{0,1:T(8,128)S(1)} %get-tuple-element.40, f32[128,4096]{0,1:T(8,128)} %copy-done.4), kind=kLoop, calls=%fused_computation | loop fusion | flops 4939776 | bytes 13172736 | tf_op jit(solution)/shard_map/concatenate | solution.py:156
  501.3 31.6 %fusion.46 = bf16[1,128,12288]{1,2,0:T(8,128)(2,1)} fusion(f32[134,12288]{0,1:T(8,128)} %pad_maximum_fusion, f32[12288]{0:T(1024)S(1)} %bitcast.244, f32[12288]{0:T(1024)S(1)} %bitcast.246, f32[12288]{0:T(1024)S(1)} %bitcast.236, f32[12288]{0:T(1024)S(1)} %bitcast.238, f32[12288]{0:T(1024)S(1)} %bitcast.240, f32[12288]{0:T(1024)S(1)} %bitcast.242, ...), kind=kLoop, calls=%fused_computation.89 | loop fusion | flops 25165824 | bytes 47529984 | tf_op jit(solution)/shard_map/broadcast_in_dim | solution.py:174
  537.5 68.2 %all-reduce.2.cloned.1.call-done = bf16[1,7,12288]{2,0,1:T(2,128)(2,1)} async-done(((bf16[1,7,12288]{2,0,1:T(2,128)(2,1)}), bf16[1,7,12288]{2,0,1:T(2,128)(2,1)}) %all-reduce.2.cloned.1.call-update) | async-done | bytes 172048 | tf_op jit(solution)/shard_map/psum | solution.py:173
  (139 shorter events, 131.3 us)
Async XLA Ops:
  7.2 14.5 %copy-start.29 = (f32[1,7,12288]{2,0,1:T(1,128)S(1)}, f32[1,7,12288]{2,0,1:T(1,128)}, u32[]{:S(2)}) copy-start(f32[1,7,12288]{2,0,1:T(1,128)} %param.7) | copy-start | bytes 1032196
  9.5 141.1 %collective-permute-start.2 = (bf16[1,128,4096]{1,2,0:T(8,128)(2,1)}, bf16[1,128,4096]{1,2,0:T(8,128)(2,1)S(1)}, u32[]{:S(2)}, u32[]{:S(2)}) collective-permute-start(bf16[1,128,4096]{1,2,0:T(8,128)(2,1)} %copy.84), channel_id=1, source_target_pairs={{0,112},{16,0},{32,16},{48,32},{64,48},{80,64},{96,80},{112,96},{1... | collective-permute-start | bytes 3145736 | tf_op jit(solution)/shard_map/ppermute | solution.py:11
  19.9 96.0 %copy-start.14 = (bf16[1,256,2048]{2,1,0:T(8,128)(2,1)S(1)}, bf16[1,256,2048]{2,1,0:T(8,128)(2,1)}, u32[]{:S(2)}) copy-start(bf16[1,256,2048]{2,1,0:T(8,128)(2,1)} %param.8) | copy-start | bytes 3145732
  19.9 84.7 %collective-permute-start = (bf16[1,128,12288]{1,2,0:T(8,128)(2,1)}, bf16[1,128,12288]{1,2,0:T(8,128)(2,1)}, u32[]{:S(2)}, u32[]{:S(2)}) collective-permute-start(bf16[1,128,12288]{1,2,0:T(8,128)(2,1)} %copy.69), channel_id=1, source_target_pairs={{0,16},{16,32},{32,48},{48,64},{64,80},{80,96},{96,112},{112,0},{1... | collective-permute-start | bytes 9437192 | tf_op jit(solution)/shard_map/ppermute | solution.py:11
  22.4 103.6 %copy-start.15 = (f32[1,1,12288]{2,0,1:T(1,128)}, f32[1,1,12288]{2,0,1:T(1,128)S(1)}, u32[]{:S(2)}) copy-start(f32[1,1,12288]{2,0,1:T(1,128)S(1)} %get-tuple-element.45) | copy-start | bytes 147460
  112.0 5.6 collective-permute-start.1
  126.0 24.6 %copy-start = (f32[134,12288]{0,1:T(8,128)}, f32[134,12288]{0,1:T(8,128)S(1)}, u32[]{:S(2)}) copy-start(f32[134,12288]{0,1:T(8,128)S(1)} %maximum_convert_fusion) | copy-start | bytes 19759108
  150.6 11.4 %copy-start.13 = (bf16[1,128,4096]{1,2,0:T(8,128)(2,1)}, bf16[1,128,4096]{1,2,0:T(8,128)(2,1)S(1)}, u32[]{:S(2)}) copy-start(bf16[1,128,4096]{1,2,0:T(8,128)(2,1)S(1)} %collective-permute-done.2) | copy-start | bytes 3145732
  153.8 20.8 %all-to-all-start.2 = ((bf16[128,16,256]{0,2,1:T(8,128)(2,1)}), bf16[128,16,256]{0,2,1:T(8,128)(2,1)S(1)}, u32[]{:S(2)}, u32[]{:S(2)}) async-start(bf16[128,16,256]{0,2,1:T(8,128)(2,1)} %bitcast.232), calls=%async_computation.2 | async-start | bytes 2097152 | tf_op jit(solution)/shard_map/all_to_all | solution.py:141
  202.8 8.7 %copy-start.7 = (f32[2,64,64,256]{3,2,0,1:T(8,128)}, f32[2,64,64,256]{3,2,0,1:T(8,128)S(1)}, u32[]{:S(2)}) copy-start(f32[2,64,64,256]{3,2,0,1:T(8,128)S(1)} %fusion.40) | copy-start | bytes 25165828
  290.1 18.2 %slice-start.3 = ((s8[8388608]{0:T(1024)(128)(4,1)}), s8[4194304]{0:T(1024)(128)(4,1)S(1)}, s32[]{:S(2)}) async-start(s8[8388608]{0:T(1024)(128)(4,1)} %bitcast.211), calls=%async_computation.8 | async-start | bytes 8388608
  294.3 14.0 %slice-start.4 = ((s8[8388608]{0:T(1024)(128)(4,1)}), s8[4194304]{0:T(1024)(128)(4,1)S(1)}, s32[]{:S(2)}) async-start(s8[8388608]{0:T(1024)(128)(4,1)} %bitcast.211), calls=%async_computation.9 | async-start | bytes 8388608
  360.6 20.5 %all-to-all-start.1 = ((bf16[16,128,256]{2,1,0:T(8,128)(2,1)}), bf16[16,128,256]{2,1,0:T(8,128)(2,1)}, u32[]{:S(2)}, u32[]{:S(2)}) async-start(bf16[16,128,256]{2,1,0:T(8,128)(2,1)} %bitcast.231), calls=%async_computation.1 | async-start | bytes 2097152 | tf_op jit(solution)/shard_map/all_to_all | solution.py:140
  367.3 238.5 %all-reduce.2.cloned.1.call-start = ((), (), s32[]{:S(2)}) async-start(), calls=%async_computation.4 | async-start | bytes 688128 | tf_op jit(solution)/shard_map/psum | solution.py:173
  375.1 11.7 %copy-start.30 = (f32[1,4096]{1,0:T(1,128)S(1)}, f32[1,4096]{1,0:T(1,128)}, u32[]{:S(2)}) copy-start(f32[1,4096]{1,0:T(1,128)} %param.9) | copy-start | bytes 49156
  390.7 16.8 %copy-start.4 = (f32[128,4096]{0,1:T(8,128)}, f32[128,4096]{0,1:T(8,128)S(1)}, u32[]{:S(2)}) copy-start(f32[128,4096]{0,1:T(8,128)S(1)} %get-tuple-element.43) | copy-start | bytes 6291460
  410.7 12.2 %copy-start.2 = (f32[128,4096]{0,1:T(8,128)S(1)}, f32[128,4096]{0,1:T(8,128)}, u32[]{:S(2)}) copy-start(f32[128,4096]{0,1:T(8,128)} %get-tuple-element.41) | copy-start | bytes 6291460
  410.7 12.2 %copy-start.5 = (f32[128,4096]{0,1:T(8,128)S(1)}, f32[128,4096]{0,1:T(8,128)}, u32[]{:S(2)}) copy-start(f32[128,4096]{0,1:T(8,128)} %copy-done.4) | copy-start | bytes 6291460
  410.7 74.7 %collective-permute-start.3 = (bf16[6,12288]{1,0:T(8,128)(2,1)S(1)}, bf16[6,12288]{1,0:T(8,128)(2,1)S(1)}, u32[]{:S(2)}, u32[]{:S(2)}) collective-permute-start(bf16[6,12288]{1,0:T(8,128)(2,1)S(1)} %copy.93), channel_id=1, source_target_pairs={{1,0},{2,1},{3,2},{4,3},{5,4},{6,5},{7,6},{8,7},{9,8},{10,9},{11,1... | collective-permute-start | bytes 442376 | tf_op jit(solution)/shard_map/ppermute | solution.py:17
  412.9 20.3 %slice-start = ((s8[12582912]{0:T(1024)(128)(4,1)}), s8[4194304]{0:T(1024)(128)(4,1)S(1)}, s32[]{:S(2)}) async-start(s8[12582912]{0:T(1024)(128)(4,1)} %bitcast.209), calls=%async_computation.5 | async-start | bytes 8388608
  412.9 20.3 %slice-start.1 = ((s8[12582912]{0:T(1024)(128)(4,1)}), s8[4194304]{0:T(1024)(128)(4,1)S(1)}, s32[]{:S(2)}) async-start(s8[12582912]{0:T(1024)(128)(4,1)} %bitcast.209), calls=%async_computation.6 | async-start | bytes 8388608
  422.9 10.3 %slice-start.2 = ((s8[12582912]{0:T(1024)(128)(4,1)}), s8[4194304]{0:T(1024)(128)(4,1)S(1)}, s32[]{:S(2)}) async-start(s8[12582912]{0:T(1024)(128)(4,1)} %bitcast.209), calls=%async_computation.7 | async-start | bytes 8388608
  455.4 7.2 %copy-start.12 = (bf16[128,4096]{0,1:T(8,128)(2,1)S(1)}, bf16[128,4096]{0,1:T(8,128)(2,1)}, u32[]{:S(2)}) copy-start(bf16[128,4096]{0,1:T(8,128)(2,1)} %get-tuple-element.44) | copy-start | bytes 3145732
  488.9 12.3 %copy-start.3 = (f32[128,4096]{0,1:T(8,128)S(1)}, f32[128,4096]{0,1:T(8,128)}, u32[]{:S(2)}) copy-start(f32[128,4096]{0,1:T(8,128)} %get-tuple-element.41) | copy-start | bytes 6291460
  488.9 12.3 %copy-start.6 = (f32[128,4096]{0,1:T(8,128)S(1)}, f32[128,4096]{0,1:T(8,128)}, u32[]{:S(2)}) copy-start(f32[128,4096]{0,1:T(8,128)} %copy-done.4) | copy-start | bytes 6291460
  488.9 12.3 %copy-start.16 = (f32[1,1,12288]{2,0,1:T(1,128)S(1)}, f32[1,1,12288]{2,0,1:T(1,128)}, u32[]{:S(2)}) copy-start(f32[1,1,12288]{2,0,1:T(1,128)} %copy-done.15) | copy-start | bytes 147460
  488.9 12.3 %copy-start.18 = (f32[1,1,12288]{2,0,1:T(1,128)S(1)}, f32[1,1,12288]{2,0,1:T(1,128)}, u32[]{:S(2)}) copy-start(f32[1,1,12288]{2,0,1:T(1,128)} %get-tuple-element.46) | copy-start | bytes 147460
  488.9 12.3 %copy-start.20 = (f32[1,1,12288]{2,0,1:T(1,128)S(1)}, f32[1,1,12288]{2,0,1:T(1,128)}, u32[]{:S(2)}) copy-start(f32[1,1,12288]{2,0,1:T(1,128)} %get-tuple-element.47) | copy-start | bytes 147460
  488.9 12.3 %copy-start.22 = (f32[1,1,12288]{2,0,1:T(1,128)S(1)}, f32[1,1,12288]{2,0,1:T(1,128)}, u32[]{:S(2)}) copy-start(f32[1,1,12288]{2,0,1:T(1,128)} %get-tuple-element.48) | copy-start | bytes 147460
  488.9 12.3 %copy-start.24 = (f32[1,1,12288]{2,0,1:T(1,128)S(1)}, f32[1,1,12288]{2,0,1:T(1,128)}, u32[]{:S(2)}) copy-start(f32[1,1,12288]{2,0,1:T(1,128)} %get-tuple-element.49) | copy-start | bytes 147460
  488.9 12.3 %copy-start.26 = (f32[1,1,12288]{2,0,1:T(1,128)S(1)}, f32[1,1,12288]{2,0,1:T(1,128)}, u32[]{:S(2)}) copy-start(f32[1,1,12288]{2,0,1:T(1,128)} %get-tuple-element.50) | copy-start | bytes 147460
  488.9 12.3 %copy-start.28 = (f32[1,1,12288]{2,0,1:T(1,128)S(1)}, f32[1,1,12288]{2,0,1:T(1,128)}, u32[]{:S(2)}) copy-start(f32[1,1,12288]{2,0,1:T(1,128)} %get-tuple-element.51) | copy-start | bytes 147460
  (14 other events, 58.1 us)
Sparse Core Ops, SparseCore 0:
  485.5 120.2 all-reduce.1
where the time goes:
time: 625 us; the launch traced here: 615 us
  other arithmetic  228 us (36%)
  waiting for transfers between devices  160 us (26%)
  matrix products  76.2 us (12%)
  local copies, waits for them, and re-layouts  72.4 us (12%)
  blocking collectives  39.5 us (6%)
  starting transfers between devices  24.3 us (4%)
  between operations  14.9 us (2%)
    ppermute x2, waiting for transfers between devices, passed_along(): return lax.ppermute(value, axis, pairs)  82.2 us
    psum x1, waiting for transfers between devices, on_device(): lax.psum(partial_kern.astype(jnp.bfloat16), 'ctx').astype(jnp.float32)  68.2 us
    dot_general x9, matrix products, contract(): return jnp.einsum(form, table, values, precision=lax.Precision.HIGH)  63.9 us
    unnamed x9, other arithmetic  52.6 us
    broadcast_in_dim x1, other arithmetic, on_device(): input_grad[None]  31.6 us
    add x1, other arithmetic, on_device(): sum((weights[offset][None, :] * padded[margin - offset:margin - offset +...  24.5 us
    reduce_sum x1, other arithmetic, on_device(): jnp.sum(jnp.stack([feat_grad * padded[margin - offset:margin - offset + t...  20.5 us
    all_to_all x1, blocking collectives, on_device(): lax.all_to_all(gated, 'ctx', split_axis=1, concat_axis=0, tiled=True)  20.2 us
  transfers between devices with their start and end apart: 7, of which 5 were waited for; matrix products, arithmetic and copies ran while one was open for 31% of the time, Pallas kernels for 0%

commit v1 on v0

--- a/solution.py
+++ b/solution.py
@@ -103,6 +103,10 @@
 
 
 def on_device(acts, cots, kern, filt, skip):
+
+    def arrange_shifts_all(array_here):
+        return jax.lax.all_gather(array_here, "ctx").sum(axis=0)
+
     source = passed_along(acts, "section", 1)[0]
     incoming = passed_along(cots, "section", -1)[0]
     taps = kern.shape[1]
@@ -170,7 +174,7 @@
         ),
         axis=1,
     )
-    kern_grad = lax.psum(partial_kern.astype(jnp.bfloat16), "ctx").astype(jnp.float32)
+    kern_grad = arrange_shifts_all(partial_kern.astype(jnp.bfloat16)).astype(jnp.float32)
     return (output[None], input_grad[None], kern_grad[None], filt_grad.T[None], skip_grad[None])
 
 

time: 625 us -> 565 us (0.904)
  the two profiles are of different devices: /device:TPU:25 before, /device:TPU:71 now
where the time goes in v1:
time: 565 us; the launch traced here: 556 us
  other arithmetic  226 us (40%)
  waiting for transfers between devices  103 us (18%)
  matrix products  76.2 us (13%)
  local copies, waits for them, and re-layouts  73.3 us (13%)
  blocking collectives  38.9 us (7%)
  starting transfers between devices  23.3 us (4%)
  between operations  14.8 us (3%)
    ppermute x2, waiting for transfers between devices, passed_along(): return lax.ppermute(value, axis, pairs)  84.2 us
    dot_general x9, matrix products, contract(): return jnp.einsum(form, table, values, precision=lax.Precision.HIGH)  63.9 us
    unnamed x9, other arithmetic  48.5 us
    broadcast_in_dim x1, other arithmetic, on_device(): input_grad[None]  32.3 us
    add x1, other arithmetic, on_device(): sum((weights[offset][None, :] * padded[margin - offset:margin - offset +...  24.5 us
    reduce_sum x1, other arithmetic, on_device(): jnp.sum(jnp.stack([feat_grad * padded[margin - offset:margin - offset + t...  21.1 us
    unnamed x76, local copies, waits for them, and re-layouts  20.5 us
    all_to_all x1, blocking collectives, on_device(): lax.all_to_all(gated, 'ctx', split_axis=1, concat_axis=0, tiled=True)  20.2 us
  transfers between devices with their start and end apart: 7, of which 5 were waited for; matrix products, arithmetic and copies ran while one was open for 24% of the time, Pallas kernels for 0%

profile of v1, /device:TPU:71, one launch (start us, length us, event | category | flops | bytes accessed | tf_op | source)
XLA Modules:
  0.0 555.6 jit_solution(8301956620550157155)
XLA Ops:
  14.1 5.1 collective-permute-start
  21.7 84.2 %collective-permute-done = bf16[1,128,12288]{1,2,0:T(8,128)(2,1)} collective-permute-done((bf16[1,128,12288]{1,2,0:T(8,128)(2,1)}, bf16[1,128,12288]{1,2,0:T(8,128)(2,1)}, u32[]{:S(2)}, u32[]{:S(2)}) %collective-permute-start) | collective-permute-done | bytes 3145760 | tf_op jit(solution)/shard_map/ppermute | solution.py:11
  128.3 24.5 %multiply_add_fusion = f32[128,12288]{0,1:T(8,128)} fusion(f32[134,12288]{0,1:T(8,128)S(1)} %maximum_convert_fusion, f32[12288]{0:T(1024)S(1)} %bitcast.247, f32[12288]{0:T(1024)S(1)} %bitcast.249, f32[12288]{0:T(1024)S(1)} %bitcast.239, f32[12288]{0:T(1024)S(1)} %bitcast.241, f32[12288]{0:T(1024)S(1)} %bitcast.243, f32[12288]{0:T(1024)S(1)} %bitcast.245, ...), kind=kLoop, calls=%fused_computation.60 | loop fusion | flops 20447232 | bytes 50675712 | tf_op jit(solution)/shard_map/add | solution.py:122
  156.0 6.8 %all-to-all-start.2 = ((bf16[128,16,256]{0,2,1:T(8,128)(2,1)}), bf16[128,16,256]{0,2,1:T(8,128)(2,1)S(1)}, u32[]{:S(2)}, u32[]{:S(2)}) async-start(bf16[128,16,256]{0,2,1:T(8,128)(2,1)} %bitcast.235), calls=%async_computation.2 | async-start | bytes 2097152 | tf_op jit(solution)/shard_map/all_to_all | solution.py:145
  168.7 10.0 %all-to-all-done.2 = bf16[128,16,256]{0,2,1:T(8,128)(2,1)S(1)} async-done(((bf16[128,16,256]{0,2,1:T(8,128)(2,1)}), bf16[128,16,256]{0,2,1:T(8,128)(2,1)S(1)}, u32[]{:S(2)}, u32[]{:S(2)}) %all-to-all-start.2) | async-done | bytes 1048608 | tf_op jit(solution)/shard_map/all_to_all | solution.py:145
  182.9 7.3 %multiply_add_fusion.5 = (f32[1,64,64,256]{3,1,2,0:T(8,128)}, f32[1,64,64,256]{3,1,2,0:T(8,128)}, f32[1,64,64,256]{3,1,2,0:T(8,128)}, f32[1,64,64,256]{3,1,2,0:T(8,128)}) fusion(f32[2,64,64,256]{3,1,2,0:T(8,128)S(1)} %convolution_add_fusion, f32[64,64]{0,1:T(8,128)S(1)} %get-tuple-element.64, f32[64,64]{0,1:T(8,128)S(1)} %get-tuple-element.65, ...), kind=kLoop, calls=%fused_computation.70 | loop fusion | flops 12582912 | bytes 33587200 | tf_op jit(solution)/shard_map/add | solution.py:77
  198.4 8.5 %fusion.40 = f32[2,64,64,256]{3,2,0,1:T(8,128)S(1)} fusion(f32[2,64,64,256,1]{3,1,2,0,4:T(8,128)S(1)} %maximum_bitcast_fusion.4, f32[1,64,2,64]{3,1,2,0:T(8,128)S(1)} %get-tuple-element.57, f32[1,64,2,64]{3,1,2,0:T(8,128)S(1)} %get-tuple-element.60), kind=kOutput, calls=%fused_computation.84 | convolution fusion | flops 1610629120 | bytes 16842752 | tf_op jit(solution)/shard_map/pqsj,skjc->pkqc/dot_general | solution.py:58
  206.9 8.7 %fusion.37 = f32[2,64,64,256]{3,2,0,1:T(8,128)S(1)} fusion(f32[2,64,64,256,1]{3,1,2,0,4:T(8,128)S(1)} %maximum_bitcast_fusion.1, f32[1,64,2,64]{3,1,2,0:T(8,128)S(1)} %get-tuple-element.57, f32[1,64,2,64]{3,1,2,0:T(8,128)S(1)} %get-tuple-element.60), kind=kOutput, calls=%fused_computation.83 | convolution fusion | flops 1610629120 | bytes 16842752 | tf_op jit(solution)/shard_map/pqsj,skjc->pkqc/dot_general | solution.py:58
  221.4 6.5 %fusion.44 = f32[64,256,2,64]{1,3,2,0:T(8,128)S(1)} fusion(f32[1,64,64,256]{3,2,0,1:T(8,128)} %get-tuple-element.23, f32[1,64,64,256]{3,2,0,1:T(8,128)} %get-tuple-element.22, f32[1,64,2,64]{3,1,2,0:T(8,128)S(1)} %get-tuple-element.61, f32[1,64,2,64]{3,1,2,0:T(8,128)S(1)} %get-tuple-element.56), kind=kOutput, calls=%fused_computation.86 | convolution fusion | flops 1612726272 | bytes 16842752 | tf_op jit(solution)/shard_map/pjsq,skqc->pkjc/dot_general | solution.py:58
  242.1 18.8 %all_to_all.52 = bf16[16,128,256]{1,2,0:T(8,128)(2,1)S(1)} all-to-all(bf16[16,128,256]{1,2,0:T(8,128)(2,1)S(1)} %fusion.48), channel_id=1, replica_groups=mesh['section'=8,'ctx'=16] {'ctx'}, dimensions={0} | all-to-all | bytes 2097152 | tf_op jit(solution)/shard_map/all_to_all | solution.py:154
  265.8 20.2 %all_to_all.53 = bf16[128,16,256]{0,2,1:T(8,128)(2,1)} all-to-all(bf16[128,16,256]{0,2,1:T(8,128)(2,1)S(1)} %bitcast.223), channel_id=1, replica_groups=mesh['section'=8,'ctx'=16] {'ctx'}, dimensions={1} | all-to-all | bytes 2097152 | tf_op jit(solution)/shard_map/all_to_all | solution.py:139
  297.8 14.0 %fusion.34 = f32[2,64,64,256]{3,2,0,1:T(8,128)} fusion(f32[2,64,64,256,1]{3,1,2,0,4:T(8,128)} %maximum_bitcast_fusion, f32[1,64,2,64]{3,1,2,0:T(8,128)S(1)} %get-tuple-element.57, f32[1,64,2,64]{3,1,2,0:T(8,128)S(1)} %get-tuple-element.60), kind=kOutput, calls=%fused_computation.82 | convolution fusion | flops 1610629120 | bytes 16842752 | tf_op jit(solution)/shard_map/pqsj,skjc->pkqc/dot_general | solution.py:58
  311.8 11.9 %multiply_add_fusion.2 = (f32[1,64,64,256]{3,2,0,1:T(8,128)}, f32[1,64,64,256]{3,2,0,1:T(8,128)}, f32[1,64,64,256]{3,2,0,1:T(8,128)}, f32[1,64,64,256]{3,2,0,1:T(8,128)}) fusion(f32[2,64,64,256]{3,2,0,1:T(8,128)S(1)} %bitcast.215, f32[2,64,64,256]{3,2,0,1:T(8,128)} %fusion.34, f32[2,64,64,256]{3,2,0,1:T(8,128)} %copy-done.6), kind=kLoop, calls=%fused_computation.64 | loop fusion | flops 12582912 | bytes 41943040 | tf_op jit(solution)/shard_map/add | solution.py:86
  323.7 6.4 %fusion.45 = f32[64,256,2,64]{1,3,2,0:T(8,128)S(1)} fusion(f32[1,64,64,256]{3,2,0,1:T(8,128)} %get-tuple-element.38, f32[1,64,64,256]{3,2,0,1:T(8,128)} %get-tuple-element.39, f32[1,64,2,64]{3,1,2,0:T(8,128)S(1)} %get-tuple-element.61, f32[1,64,2,64]{3,1,2,0:T(8,128)S(1)} %get-tuple-element.56), kind=kOutput, calls=%fused_computation.87 | convolution fusion | flops 1612726272 | bytes 16842752 | tf_op jit(solution)/shard_map/pjsq,skqc->pkjc/dot_general | solution.py:58
  335.0 6.5 %fusion.43 = f32[64,256,2,64]{1,3,2,0:T(8,128)S(1)} fusion(f32[1,64,64,256]{3,2,0,1:T(8,128)} %get-tuple-element.21, f32[1,64,64,256]{3,2,0,1:T(8,128)} %get-tuple-element.20, f32[1,64,2,64]{3,1,2,0:T(8,128)S(1)} %get-tuple-element.61, f32[1,64,2,64]{3,1,2,0:T(8,128)S(1)} %get-tuple-element.56), kind=kOutput, calls=%fused_computation.85 | convolution fusion | flops 1612726272 | bytes 16842752 | tf_op jit(solution)/shard_map/pjsq,skqc->pkjc/dot_general | solution.py:58
  341.4 8.2 %copy.163 = f32[64,256,2,64]{1,0,3,2:T(8,128)} copy(f32[64,256,2,64]{1,3,2,0:T(8,128)S(1)} %fusion.43) | data formatting | bytes 16777216 | tf_op jit(solution)/shard_map/pjsq,skqc->pkjc/dot_general | solution.py:58
  349.6 7.8 %multiply_subtract_fusion = (f32[1,64,64,256]{3,1,2,0:T(8,128)}, f32[1,64,64,256]{3,1,2,0:T(8,128)}, f32[1,64,64,256]{3,1,2,0:T(8,128)S(1)}, f32[1,64,64,256]{3,1,2,0:T(8,128)}) fusion(f32[2,64,64,256]{3,1,2,0:T(8,128)} %bitcast.220, f32[64,64]{0,1:T(8,128)S(1)} %get-tuple-element.64, f32[64,64]{0,1:T(8,128)S(1)} %get-tuple-element.65, ...), kind=kLoop, calls=%fused_computation.62 | loop fusion | flops 12582912 | bytes 33587200 | tf_op jit(solution)/shard_map/sub | solution.py:99
  357.4 5.1 fusion.51
  364.2 5.1 all-to-all-start.1
  369.4 5.3 bitcast_multiply_fusion
  380.1 5.3 all-to-all-done.1
  395.2 11.6 %bitcast_dynamic-update-slice_fusion.6 = f32[7,128,12288]{1,2,0:T(8,128)} fusion(f32[134,12288]{0,1:T(8,128)} %copy-done, f32[128,4096]{0,1:T(8,128)S(1)} %copy-done.1, f32[128,4096]{0,1:T(8,128)S(1)} %get-tuple-element.40, f32[128,4096]{0,1:T(8,128)S(1)} %get-tuple-element.43), kind=kLoop, calls=%fused_computation.59 | loop fusion | flops 4718591 | bytes 18874368
  406.9 7.4 %bitcast_dynamic-update-slice_fusion.5 = f32[7,128,12288]{1,2,0:T(8,128)} fusion(f32[7,128,12288]{1,2,0:T(8,128)} %bitcast_dynamic-update-slice_fusion.6, f32[134,12288]{0,1:T(8,128)S(1)} %bitcast.213, f32[128,4096]{0,1:T(8,128)S(1)} %copy-done.1, f32[128,4096]{0,1:T(8,128)S(1)} %get-tuple-element.40, f32[128,4096]{0,1:T(8,128)S(1)} %get-tuple-element.43), kind=kLoop, calls=%fused_computation.58 | loop fusion | flops 4718592 | bytes 18874368
  414.3 7.5 %bitcast_dynamic-update-slice_fusion.4 = f32[7,128,12288]{1,2,0:T(8,128)} fusion(f32[7,128,12288]{1,2,0:T(8,128)} %bitcast_dynamic-update-slice_fusion.5, f32[134,12288]{0,1:T(8,128)S(1)} %bitcast.213, f32[128,4096]{0,1:T(8,128)S(1)} %copy-done.1, f32[128,4096]{0,1:T(8,128)S(1)} %get-tuple-element.40, f32[128,4096]{0,1:T(8,128)S(1)} %get-tuple-element.43), kind=kLoop, calls=%fused_computation.57 | loop fusion | flops 4718592 | bytes 18874368
  421.7 7.3 %bitcast_dynamic-update-slice_fusion.3 = f32[7,128,12288]{1,2,0:T(8,128)} fusion(f32[7,128,12288]{1,2,0:T(8,128)} %bitcast_dynamic-update-slice_fusion.4, f32[134,12288]{0,1:T(8,128)S(1)} %bitcast.213, f32[128,4096]{0,1:T(8,128)S(1)} %copy-done.1, f32[128,4096]{0,1:T(8,128)S(1)} %get-tuple-element.40, f32[128,4096]{0,1:T(8,128)S(1)} %get-tuple-element.43), kind=kLoop, calls=%fused_computation.56 | loop fusion | flops 4718592 | bytes 18874368
  429.1 7.3 %bitcast_dynamic-update-slice_fusion.2 = f32[7,128,12288]{1,2,0:T(8,128)} fusion(f32[7,128,12288]{1,2,0:T(8,128)} %bitcast_dynamic-update-slice_fusion.3, f32[134,12288]{0,1:T(8,128)S(1)} %bitcast.213, f32[128,4096]{0,1:T(8,128)S(1)} %copy-done.1, f32[128,4096]{0,1:T(8,128)S(1)} %get-tuple-element.40, f32[128,4096]{0,1:T(8,128)S(1)} %get-tuple-element.43), kind=kLoop, calls=%fused_computation.55 | loop fusion | flops 4718592 | bytes 18874368
  436.4 7.3 %bitcast_dynamic-update-slice_fusion.1 = f32[7,128,12288]{1,2,0:T(8,128)} fusion(f32[7,128,12288]{1,2,0:T(8,128)} %bitcast_dynamic-update-slice_fusion.2, f32[134,12288]{0,1:T(8,128)S(1)} %bitcast.213, f32[128,4096]{0,1:T(8,128)S(1)} %copy-done.1, f32[128,4096]{0,1:T(8,128)S(1)} %get-tuple-element.40, f32[128,4096]{0,1:T(8,128)S(1)} %get-tuple-element.43), kind=kLoop, calls=%fused_computation.54 | loop fusion | flops 4718592 | bytes 18874368
  443.7 7.4 %bitcast_dynamic-update-slice_fusion = f32[7,128,12288]{1,2,0:T(8,128)} fusion(f32[7,128,12288]{1,2,0:T(8,128)} %bitcast_dynamic-update-slice_fusion.1, f32[134,12288]{0,1:T(8,128)S(1)} %bitcast.213, f32[128,4096]{0,1:T(8,128)S(1)} %copy-done.1, f32[128,4096]{0,1:T(8,128)S(1)} %get-tuple-element.40, f32[128,4096]{0,1:T(8,128)S(1)} %get-tuple-element.43), kind=kLoop, calls=%fused_computation.53 | loop fusion | flops 4718592 | bytes 18874368 | tf_op jit(solution)/shard_map/stack | solution.py:168
  451.1 21.1 %reduce_sum.30 = bf16[7,12288]{1,0:T(8,128)(2,1)} reduce(f32[7,128,12288]{1,2,0:T(8,128)} %bitcast_dynamic-update-slice_fusion, f32[]{:T(128)} %constant.56.clone.1), dimensions={1}, to_apply=%region_0.1 | reduce | flops 10924032 | bytes 44212228 | tf_op jit(solution)/shard_map/reduce_sum | solution.py:167
  472.3 6.3 %pad_maximum_fusion.1 = bf16[128,12288]{0,1:T(8,128)(2,1)} fusion(f32[128,4096]{0,1:T(8,128)} %get-tuple-element.41, f32[128,4096]{0,1:T(8,128)S(1)} %get-tuple-element.40, f32[128,4096]{0,1:T(8,128)} %copy-done.3), kind=kLoop, calls=%fused_computation.52 | loop fusion | flops 9437184 | bytes 9437184 | tf_op jit(solution)/shard_map/concatenate | solution.py:158
  495.6 12.4 %pad_maximum_fusion = f32[134,12288]{0,1:T(8,128)} fusion(f32[6,12288]{0,1:T(8,128)} %copy.94, f32[128,4096]{0,1:T(8,128)} %get-tuple-element.41, f32[128,4096]{0,1:T(8,128)S(1)} %get-tuple-element.40, f32[128,4096]{0,1:T(8,128)} %copy-done.3), kind=kLoop, calls=%fused_computation | loop fusion | flops 4939776 | bytes 13172736 | tf_op jit(solution)/shard_map/concatenate | solution.py:160
  508.1 32.3 %fusion.46 = bf16[1,128,12288]{1,2,0:T(8,128)(2,1)} fusion(f32[134,12288]{0,1:T(8,128)} %pad_maximum_fusion, f32[12288]{0:T(1024)S(1)} %bitcast.248, f32[12288]{0:T(1024)S(1)} %bitcast.250, f32[12288]{0:T(1024)S(1)} %bitcast.240, f32[12288]{0:T(1024)S(1)} %bitcast.242, f32[12288]{0:T(1024)S(1)} %bitcast.244, f32[12288]{0:T(1024)S(1)} %bitcast.246, ...), kind=kLoop, calls=%fused_computation.89 | loop fusion | flops 25165824 | bytes 47529984 | tf_op jit(solution)/shard_map/broadcast_in_dim | solution.py:178
  (131 shorter events, 136.6 us)
Async XLA Ops:
  7.2 13.8 %copy-start.25 = (f32[1,7,12288]{2,0,1:T(1,128)S(1)}, f32[1,7,12288]{2,0,1:T(1,128)}, u32[]{:S(2)}) copy-start(f32[1,7,12288]{2,0,1:T(1,128)} %param.7) | copy-start | bytes 1032196
  9.5 143.3 %collective-permute-start.2 = (bf16[1,128,4096]{1,2,0:T(8,128)(2,1)}, bf16[1,128,4096]{1,2,0:T(8,128)(2,1)S(1)}, u32[]{:S(2)}, u32[]{:S(2)}) collective-permute-start(bf16[1,128,4096]{1,2,0:T(8,128)(2,1)} %copy.84), channel_id=1, source_target_pairs={{0,112},{16,0},{32,16},{48,32},{64,48},{80,64},{96,80},{112,96},{1... | collective-permute-start | bytes 3145736 | tf_op jit(solution)/shard_map/ppermute | solution.py:11
  14.1 104.1 %copy-start.10 = (bf16[1,256,2048]{2,1,0:T(8,128)(2,1)S(1)}, bf16[1,256,2048]{2,1,0:T(8,128)(2,1)}, u32[]{:S(2)}) copy-start(bf16[1,256,2048]{2,1,0:T(8,128)(2,1)} %param.8) | copy-start | bytes 3145732
  14.1 91.8 %collective-permute-start = (bf16[1,128,12288]{1,2,0:T(8,128)(2,1)}, bf16[1,128,12288]{1,2,0:T(8,128)(2,1)}, u32[]{:S(2)}, u32[]{:S(2)}) collective-permute-start(bf16[1,128,12288]{1,2,0:T(8,128)(2,1)} %copy.69), channel_id=1, source_target_pairs={{0,16},{16,32},{32,48},{48,64},{64,80},{80,96},{96,112},{112,0},{1... | collective-permute-start | bytes 9437192 | tf_op jit(solution)/shard_map/ppermute | solution.py:11
  21.7 106.5 %copy-start.11 = (f32[1,1,12288]{2,0,1:T(1,128)}, f32[1,1,12288]{2,0,1:T(1,128)S(1)}, u32[]{:S(2)}) copy-start(f32[1,1,12288]{2,0,1:T(1,128)S(1)} %get-tuple-element.45) | copy-start | bytes 147460
  113.3 6.5 %collective-permute-start.1 = (bf16[6,12288]{1,0:T(8,128)(2,1)}, bf16[6,12288]{1,0:T(8,128)(2,1)}, u32[]{:S(2)}, u32[]{:S(2)}) collective-permute-start(bf16[6,12288]{1,0:T(8,128)(2,1)} %copy.70), channel_id=1, source_target_pairs={{0,1},{1,2},{2,3},{3,4},{4,5},{5,6},{6,7},{7,8},{8,9},{9,10},{10,1... | collective-permute-start | bytes 442376 | tf_op jit(solution)/shard_map/ppermute | solution.py:17
  123.5 4.8 copy-start.21
  123.5 4.8 copy-start.23
  128.2 24.6 %copy-start = (f32[134,12288]{0,1:T(8,128)}, f32[134,12288]{0,1:T(8,128)S(1)}, u32[]{:S(2)}) copy-start(f32[134,12288]{0,1:T(8,128)S(1)} %maximum_convert_fusion) | copy-start | bytes 19759108
  152.8 11.3 %copy-start.9 = (bf16[1,128,4096]{1,2,0:T(8,128)(2,1)}, bf16[1,128,4096]{1,2,0:T(8,128)(2,1)S(1)}, u32[]{:S(2)}) copy-start(bf16[1,128,4096]{1,2,0:T(8,128)(2,1)S(1)} %collective-permute-done.2) | copy-start | bytes 3145732
  156.0 22.7 %all-to-all-start.2 = ((bf16[128,16,256]{0,2,1:T(8,128)(2,1)}), bf16[128,16,256]{0,2,1:T(8,128)(2,1)S(1)}, u32[]{:S(2)}, u32[]{:S(2)}) async-start(bf16[128,16,256]{0,2,1:T(8,128)(2,1)} %bitcast.235), calls=%async_computation.2 | async-start | bytes 2097152 | tf_op jit(solution)/shard_map/all_to_all | solution.py:145
  206.9 8.7 %copy-start.5 = (f32[2,64,64,256]{3,2,0,1:T(8,128)}, f32[2,64,64,256]{3,2,0,1:T(8,128)S(1)}, u32[]{:S(2)}) copy-start(f32[2,64,64,256]{3,2,0,1:T(8,128)S(1)} %fusion.40) | copy-start | bytes 25165828
  215.6 5.8 %copy-start.6 = (f32[2,64,64,256]{3,2,0,1:T(8,128)}, f32[2,64,64,256]{3,2,0,1:T(8,128)S(1)}, u32[]{:S(2)}) copy-start(f32[2,64,64,256]{3,2,0,1:T(8,128)S(1)} %fusion.37) | copy-start | bytes 25165828
  293.7 18.1 %slice-start.3 = ((s8[8388608]{0:T(1024)(128)(4,1)}), s8[4194304]{0:T(1024)(128)(4,1)S(1)}, s32[]{:S(2)}) async-start(s8[8388608]{0:T(1024)(128)(4,1)} %bitcast.214), calls=%async_computation.8 | async-start | bytes 8388608
  297.8 14.0 %slice-start.4 = ((s8[8388608]{0:T(1024)(128)(4,1)}), s8[4194304]{0:T(1024)(128)(4,1)S(1)}, s32[]{:S(2)}) async-start(s8[8388608]{0:T(1024)(128)(4,1)} %bitcast.214), calls=%async_computation.9 | async-start | bytes 8388608
  364.2 21.2 %all-to-all-start.1 = ((bf16[16,128,256]{2,1,0:T(8,128)(2,1)}), bf16[16,128,256]{2,1,0:T(8,128)(2,1)}, u32[]{:S(2)}, u32[]{:S(2)}) async-start(bf16[16,128,256]{2,1,0:T(8,128)(2,1)} %bitcast.234), calls=%async_computation.1 | async-start | bytes 2097152 | tf_op jit(solution)/shard_map/all_to_all | solution.py:144
  369.3 175.7 %all-gather.4.cloned.1.call-start = ((), (), s32[]{:S(2)}) async-start(), calls=%async_computation.4 | async-start | bytes 3342336 | tf_op jit(solution)/shard_map/all_gather | solution.py:108
  377.2 13.9 %copy-start.26 = (f32[1,4096]{1,0:T(1,128)S(1)}, f32[1,4096]{1,0:T(1,128)}, u32[]{:S(2)}) copy-start(f32[1,4096]{1,0:T(1,128)} %param.9) | copy-start | bytes 49156
  391.1 15.8 %slice-start = ((s8[12582912]{0:T(1024)(128)(4,1)}), s8[4194304]{0:T(1024)(128)(4,1)S(1)}, s32[]{:S(2)}) async-start(s8[12582912]{0:T(1024)(128)(4,1)} %bitcast.212), calls=%async_computation.5 | async-start | bytes 8388608
  391.1 15.8 %slice-start.1 = ((s8[12582912]{0:T(1024)(128)(4,1)}), s8[4194304]{0:T(1024)(128)(4,1)S(1)}, s32[]{:S(2)}) async-start(s8[12582912]{0:T(1024)(128)(4,1)} %bitcast.212), calls=%async_computation.6 | async-start | bytes 8388608
  395.2 48.5 %copy-start.3 = (f32[128,4096]{0,1:T(8,128)}, f32[128,4096]{0,1:T(8,128)S(1)}, u32[]{:S(2)}) copy-start(f32[128,4096]{0,1:T(8,128)S(1)} %get-tuple-element.43) | copy-start | bytes 6291460
  395.2 11.7 %slice-start.2 = ((s8[12582912]{0:T(1024)(128)(4,1)}), s8[4194304]{0:T(1024)(128)(4,1)S(1)}, s32[]{:S(2)}) async-start(s8[12582912]{0:T(1024)(128)(4,1)} %bitcast.212), calls=%async_computation.7 | async-start | bytes 8388608
  481.8 10.2 %collective-permute-start.3 = (bf16[6,12288]{1,0:T(8,128)(2,1)S(1)}, bf16[6,12288]{1,0:T(8,128)(2,1)S(1)}, u32[]{:S(2)}, u32[]{:S(2)}) collective-permute-start(bf16[6,12288]{1,0:T(8,128)(2,1)S(1)} %copy.93), channel_id=1, source_target_pairs={{1,0},{2,1},{3,2},{4,3},{5,4},{6,5},{7,6},{8,7},{9,8},{10,9},{11,1... | collective-permute-start | bytes 442376 | tf_op jit(solution)/shard_map/ppermute | solution.py:17
  495.6 12.4 %copy-start.2 = (f32[128,4096]{0,1:T(8,128)S(1)}, f32[128,4096]{0,1:T(8,128)}, u32[]{:S(2)}) copy-start(f32[128,4096]{0,1:T(8,128)} %get-tuple-element.41) | copy-start | bytes 6291460
  495.6 12.4 %copy-start.4 = (f32[128,4096]{0,1:T(8,128)S(1)}, f32[128,4096]{0,1:T(8,128)}, u32[]{:S(2)}) copy-start(f32[128,4096]{0,1:T(8,128)} %copy-done.3) | copy-start | bytes 6291460
  495.6 12.4 %copy-start.12 = (f32[1,1,12288]{2,0,1:T(1,128)S(1)}, f32[1,1,12288]{2,0,1:T(1,128)}, u32[]{:S(2)}) copy-start(f32[1,1,12288]{2,0,1:T(1,128)} %copy-done.11) | copy-start | bytes 147460
  495.6 12.4 %copy-start.14 = (f32[1,1,12288]{2,0,1:T(1,128)S(1)}, f32[1,1,12288]{2,0,1:T(1,128)}, u32[]{:S(2)}) copy-start(f32[1,1,12288]{2,0,1:T(1,128)} %get-tuple-element.46) | copy-start | bytes 147460
  495.6 12.4 %copy-start.16 = (f32[1,1,12288]{2,0,1:T(1,128)S(1)}, f32[1,1,12288]{2,0,1:T(1,128)}, u32[]{:S(2)}) copy-start(f32[1,1,12288]{2,0,1:T(1,128)} %get-tuple-element.47) | copy-start | bytes 147460
  495.6 12.4 %copy-start.18 = (f32[1,1,12288]{2,0,1:T(1,128)S(1)}, f32[1,1,12288]{2,0,1:T(1,128)}, u32[]{:S(2)}) copy-start(f32[1,1,12288]{2,0,1:T(1,128)} %get-tuple-element.48) | copy-start | bytes 147460
  495.6 12.4 %copy-start.20 = (f32[1,1,12288]{2,0,1:T(1,128)S(1)}, f32[1,1,12288]{2,0,1:T(1,128)}, u32[]{:S(2)}) copy-start(f32[1,1,12288]{2,0,1:T(1,128)} %get-tuple-element.49) | copy-start | bytes 147460
  495.6 12.4 %copy-start.22 = (f32[1,1,12288]{2,0,1:T(1,128)S(1)}, f32[1,1,12288]{2,0,1:T(1,128)}, u32[]{:S(2)}) copy-start(f32[1,1,12288]{2,0,1:T(1,128)} %get-tuple-element.50) | copy-start | bytes 147460
  495.6 12.4 %copy-start.24 = (f32[1,1,12288]{2,0,1:T(1,128)S(1)}, f32[1,1,12288]{2,0,1:T(1,128)}, u32[]{:S(2)}) copy-start(f32[1,1,12288]{2,0,1:T(1,128)} %get-tuple-element.51) | copy-start | bytes 147460
  (10 other events, 36.3 us)
Sparse Core Ops, SparseCore 0:
  472.4 35.2 all-gather.3
